TPU v7x, 512 devices: a whole 4x8x8 slice. The times are simulated.
512 devices in a mesh: front: 4 (over x), row: 8 (over y), col: 16 (over z, core).
Axes of the slice: x: 4, y: 8, z: 8, core: 2. Of those that a mesh axis runs over, the one named last changes fastest.
Arguments:
- contrib: float32 [32768, 4096], P(('front', 'row'), 'col'), parts along dimension 0, as said below
- front_diag: float32 [32768], P(('front', 'row')), parts along dimension 0, may hold values from 1 to 4
- child_map: int32 [8, 32], P('front'), parts along dimension 0, may hold values from 0 to 63, as said below
- pivots: int32 [16], P('front'), parts along dimension 0, may hold values from 0 to 63, as said below
Outputs:
- lfactor: float32 [32768, 512], P(('front', 'row'), 'col'), parts along dimension 0
- schur_block: float32 [32768, 8192], P(('front', 'row'), 'col'), parts along dimension 0
There are 4 independent parts, one for each index of `front`. A program takes and returns all parts, laid end to end along the dimension named above; each array names one. Nothing has to cross between parts.
Inputs may be any that keep to these rules, and one draw needn't show every extreme that they name: child_map[c, b] is b or b + 32, chosen for each child and block. `pivots`: 4 distinct front blocks. `contrib`: each child's contribution block is symmetric positive definite.
All inputs are finite; a program needn't handle non-finite values.
Results may differ from a plain program's by a relative error of at most 0.0001.
Values sent between devices are 32-bit elements; how exact they have to be, the bound alone decides.
A program may use at most 64 MiB of HBM per device.

v0:
```python
import jax
import jax.numpy as jnp
from jax import lax
from jax.sharding import PartitionSpec as P

NF = 8192
NPAN = 2
BLK = 128
highest = lax.Precision.HIGHEST


def swapped(shard, axis, bit):
    return lax.ppermute(shard, axis, [(i, i ^ 1 << bit) for i in range(lax.axis_size(axis))])


def broadcast(shard, axis, root):
    mine = lax.axis_index(axis) == root
    return lax.psum(jnp.where(mine, shard, jnp.zeros_like(shard)), axis)


def select_rows(mapping, chosen_ids, within, half_rows, row_index, row_count, row_slots):
    by_device = mapping.reshape(mapping.shape[0] // half_rows, half_rows)
    targets = jnp.take(lax.dynamic_index_in_dim(by_device, within, 1, keepdims=False), chosen_ids)
    slot_ids = jnp.arange(row_slots) * row_count + row_index
    return (targets[None, :] == slot_ids[:, None]).astype(jnp.float32)


def select_cols(mapping, col_index, col_count, col_slots):
    by_device = mapping.reshape(mapping.shape[0] // col_count, col_count)
    targets = lax.dynamic_index_in_dim(by_device, col_index, 1, keepdims=False)
    slot_ids = jnp.arange(col_slots) * col_count + col_index
    return (targets[None, :] == slot_ids[:, None]).astype(jnp.float32)


def place_blocks(pieces, row_select, col_select):
    blocks = pieces.reshape(row_select.shape[1], BLK, col_select.shape[1], BLK)
    placed = jnp.einsum("kj,jaib->kaib", row_select, blocks, precision=highest)
    placed = jnp.einsum("li,kaib->kalb", col_select, placed, precision=highest)
    return placed.reshape(row_select.shape[0] * BLK, col_select.shape[0] * BLK)


def per_device(contrib, front_diag, child_map, pivots):
    row_count = lax.axis_size("row")
    col_count = lax.axis_size("col")
    row_index = lax.axis_index("row")
    col_index = lax.axis_index("col")
    half_rows = row_count // 2
    half_bit = half_rows.bit_length() - 1
    sibling = row_index // half_rows
    within = row_index % half_rows
    local_rows = front_diag.shape[0]
    row_slots = local_rows // BLK
    col_width = NF // col_count
    col_slots = col_width // BLK
    child_rows = contrib.shape[0] // BLK
    own_map = lax.dynamic_index_in_dim(child_map, sibling, 0, keepdims=False)
    other_map = lax.dynamic_index_in_dim(child_map, 1 - sibling, 0, keepdims=False)
    partner = swapped(contrib, "row", half_bit)
    other_ids = jnp.arange(child_rows)
    own_rows = select_rows(
        own_map, jnp.arange(child_rows), within, half_rows, row_index, row_count, row_slots
    )
    other_rows = select_rows(
        other_map, other_ids, within, half_rows, row_index, row_count, row_slots
    )
    own_cols = select_cols(own_map, col_index, col_count, col_slots)
    other_cols = select_cols(other_map, col_index, col_count, col_slots)
    assembled = place_blocks(contrib, own_rows, own_cols) + place_blocks(
        partner, other_rows, other_cols
    )
    row_ids = jnp.arange(row_slots) * row_count + row_index
    col_ids = jnp.arange(col_slots) * col_count + col_index
    on_diagonal = (row_ids[:, None] == col_ids[None, :]).astype(jnp.float32)
    identity = jnp.eye(BLK, dtype=jnp.float32)
    diag_blocks = front_diag.reshape(row_slots, BLK)
    diag_part = (
        on_diagonal[:, None, :, None] * diag_blocks[:, :, None, None] * identity[None, :, None, :]
    )
    front_tile = assembled + diag_part.reshape(local_rows, col_width)
    factors = []
    for panel_index in range(NPAN):
        chosen = [pivots[2 * panel_index], pivots[2 * panel_index + 1]]
        columns = []
        for block_id in chosen:
            block_piece = lax.dynamic_slice_in_dim(front_tile, block_id // col_count * BLK, BLK, 1)
            columns.append(broadcast(block_piece, "col", block_id % col_count))
        panel_cols = jnp.concatenate(columns, axis=1)
        owned_rows = []
        for block_id in chosen:
            rows_here = lax.dynamic_slice_in_dim(panel_cols, block_id // row_count * BLK, BLK, 0)
            owned_rows.append(jnp.where(block_id % row_count == row_index, rows_here, 0.0))
        pivot_block = lax.psum(jnp.concatenate(owned_rows, axis=0), "row")
        lower_factor = jnp.linalg.cholesky(pivot_block)
        factor = lax.linalg.triangular_solve(
            lower_factor, panel_cols, left_side=False, lower=True, transpose_a=True
        )
        source_rows = []
        for slot_index in range(col_slots):
            source_rows.append(
                lax.dynamic_slice_in_dim(factor, col_ids[slot_index] // row_count * BLK, BLK, 0)
            )
        across = broadcast(jnp.concatenate(source_rows, axis=0), "row", col_index % row_count)
        update = jnp.einsum("ak,bk->ab", factor, across, precision=highest)
        row_hit = jnp.logical_or(row_ids == chosen[0], row_ids == chosen[1])
        col_hit = jnp.logical_or(col_ids == chosen[0], col_ids == chosen[1])
        row_keep = jnp.repeat(jnp.where(row_hit, 0.0, 1.0), BLK)
        col_keep = jnp.repeat(jnp.where(col_hit, 0.0, 1.0), BLK)
        front_tile = (front_tile - update) * row_keep[:, None] * col_keep[None, :]
        factors.append(factor)
    stacked = jnp.concatenate(factors, axis=1)
    col_share = stacked.shape[1] // col_count
    lfactor = lax.dynamic_slice_in_dim(stacked, col_index * col_share, col_share, 1)
    return (lfactor, front_tile)


def solution(mesh):
    placed = (P(("front", "row"), "col"), P(("front", "row")), P("front", None), P("front"))
    return jax.shard_map(
        per_device,
        mesh=mesh,
        in_specs=placed,
        out_specs=(P(("front", "row"), "col"), P(("front", "row"), "col")),
        check_vma=False,
    )
```

profile of v0, /device:TPU:2, one launch (start us, length us, event | category | flops | bytes accessed | tf_op | source)
XLA Modules:
  0.0 781.1 jit_solution(6074221105859730015)
XLA Ops:
  7.2 7.7 collective-permute-start
  17.5 1.4 fusion.61
  19.0 1.7 reshape.126
  26.9 1.2 fusion.5
  28.0 2.3 fusion.3
  30.4 30.0 %collective-permute-done = f32[1024,256]{1,0:T(8,128)} collective-permute-done((f32[1024,256]{1,0:T(8,128)}, f32[1024,256]{1,0:T(8,128)}, u32[]{:S(2)}, u32[]{:S(2)}) %collective-permute-start) | collective-permute-done | bytes 1048608 | tf_op jit(solution)/shard_map/ppermute | solution.py:13
  60.4 1.7 reshape.129
  62.1 1.2 fusion.1
  63.3 3.7 bitcast_add_fusion
  67.0 1.5 copy.39
  68.5 1.9 copy.28
  70.4 1.2 dynamic-slice_select_fusion.2
  71.7 123.2 %all-reduce.20.cloned.1.call-done = (f32[1024,128]{0,1:T(8,128)}, f32[1024,128]{0,1:T(8,128)}) async-done(((f32[1024,128]{0,1:T(8,128)}, f32[1024,128]{0,1:T(8,128)}), (f32[1024,128]{0,1:T(8,128)}, f32[1024,128]{0,1:T(8,128)})) %all-reduce.20.cloned.1.call-update) | async-done | bytes 1048592 | tf_op jit(solution)/shard_map/psum | solution.py:18
  195.0 1.1 constant_dynamic-update-slice_fusion.3
  196.1 1.1 constant_dynamic-update-slice_fusion.2
  213.8 1.2 or_select_fusion.2
  215.0 60.4 %all-reduce.10.cloned.1.call-done = f32[256,256]{0,1:T(8,128)} async-done(((f32[256,256]{0,1:T(8,128)}), f32[256,256]{0,1:T(8,128)}) %all-reduce.10.cloned.1.call-update) | async-done | bytes 262160 | tf_op jit(solution)/shard_map/psum | solution.py:92
  275.4 1.1 copy.13
  277.5 11.7 %cholesky.130 = f32[128,128]{1,0:T(8,128)S(1)} custom-call(f32[128,128]{1,0:T(8,128)S(1)} %cholesky.194), custom_call_target="Cholesky" | custom-call | tf_op jit(solution)/shard_map/jit(cholesky)/cholesky | solution.py:93
  289.2 9.8 %custom-call.13 = f32[1,128,128]{1,2,0:T(8,128)S(1)} custom-call(f32[1,128,128]{2,1,0:T(8,128)S(1)} %get-tuple-element.74), custom_call_target="InvertDiagBlocksLowerTriangular" | custom-call | tf_op jit(solution)/shard_map/jit(cholesky)/cholesky | solution.py:93
  299.5 11.7 %cholesky.147 = f32[128,128]{1,0:T(8,128)S(1)} custom-call(f32[128,128]{1,0:T(8,128)S(1)} %convolution_subtract_fusion.3), custom_call_target="Cholesky" | custom-call | tf_op jit(solution)/shard_map/jit(cholesky)/cholesky | solution.py:93
  314.0 4.3 while.4
  314.9 1.4 bitcast_dynamic-update-slice_fusion.4
  317.0 1.4 bitcast_dynamic-update-slice_fusion.4
  318.4 19.7 %custom-call.14 = f32[2,128,128]{1,2,0:T(8,128)S(1)} custom-call(f32[2,128,128]{2,1,0:T(8,128)S(1)} %get-tuple-element.19), custom_call_target="InvertDiagBlocksLowerTriangular" | custom-call | tf_op jit(solution)/shard_map/triangular_solve/custom-call.0 | solution.py:94
  341.0 1.2 or_select_fusion.3
  342.3 76.2 %all-reduce.12.cloned.1.call-done = f32[512,256]{0,1:T(8,128)} async-done(((f32[512,256]{0,1:T(8,128)}), f32[512,256]{0,1:T(8,128)}) %all-reduce.12.cloned.1.call-update) | async-done | bytes 524304 | tf_op jit(solution)/shard_map/psum | solution.py:18
  418.5 3.8 multiply_multiply_fusion.1
  422.3 1.1 dynamic-slice_select_fusion.1
  423.5 116.7 %all-reduce.18.cloned.1.call-done = (f32[1024,128]{0,1:T(8,128)}, f32[1024,128]{0,1:T(8,128)}) async-done(((f32[1024,128]{0,1:T(8,128)}, f32[1024,128]{0,1:T(8,128)}), (f32[1024,128]{0,1:T(8,128)}, f32[1024,128]{0,1:T(8,128)})) %all-reduce.18.cloned.1.call-update) | async-done | bytes 1048592 | tf_op jit(solution)/shard_map/psum | solution.py:18
  540.2 1.1 constant_dynamic-update-slice_fusion.5
  541.3 1.1 constant_dynamic-update-slice_fusion.4
  543.5 1.2 or_select_fusion
  544.7 1.2 or_select_fusion.1
  546.0 74.6 %all-reduce.14.cloned.1.call-done = f32[256,256]{0,1:T(8,128)} async-done(((f32[256,256]{0,1:T(8,128)}), f32[256,256]{0,1:T(8,128)}) %all-reduce.14.cloned.1.call-update) | async-done | bytes 262160 | tf_op jit(solution)/shard_map/psum | solution.py:92
  620.6 1.1 copy.15
  622.7 11.7 %cholesky.164 = f32[128,128]{1,0:T(8,128)S(1)} custom-call(f32[128,128]{1,0:T(8,128)S(1)} %cholesky.197), custom_call_target="Cholesky" | custom-call | tf_op jit(solution)/shard_map/jit(cholesky)/cholesky | solution.py:93
  634.4 9.8 %custom-call.15 = f32[1,128,128]{1,2,0:T(8,128)S(1)} custom-call(f32[1,128,128]{2,1,0:T(8,128)S(1)} %get-tuple-element.70), custom_call_target="InvertDiagBlocksLowerTriangular" | custom-call | tf_op jit(solution)/shard_map/jit(cholesky)/cholesky | solution.py:93
  644.7 11.7 %cholesky.181 = f32[128,128]{1,0:T(8,128)S(1)} custom-call(f32[128,128]{1,0:T(8,128)S(1)} %convolution_subtract_fusion.2), custom_call_target="Cholesky" | custom-call | tf_op jit(solution)/shard_map/jit(cholesky)/cholesky | solution.py:93
  659.1 4.2 while.5
  660.0 1.3 bitcast_dynamic-update-slice_fusion.5
  662.0 1.3 bitcast_dynamic-update-slice_fusion.5
  663.3 19.7 %custom-call.16 = f32[2,128,128]{1,2,0:T(8,128)S(1)} custom-call(f32[2,128,128]{2,1,0:T(8,128)S(1)} %get-tuple-element.20), custom_call_target="InvertDiagBlocksLowerTriangular" | custom-call | tf_op jit(solution)/shard_map/triangular_solve/custom-call.0 | solution.py:94
  683.0 1.7 fusion.22
  684.7 1.7 convolution_subtract_fusion
  689.5 76.7 %all-reduce.16.cloned.1.call-done = f32[512,256]{0,1:T(8,128)} async-done(((f32[512,256]{0,1:T(8,128)}), f32[512,256]{0,1:T(8,128)}) %all-reduce.16.cloned.1.call-update) | async-done | bytes 524304 | tf_op jit(solution)/shard_map/psum | solution.py:18
  766.2 4.6 multiply_multiply_fusion
  770.8 2.9 copy.17
  (94 shorter events, 21.5 us)
Async XLA Ops:
  7.2 18.7 %copy-start.6 = (f32[1024]{0:T(1024)S(1)}, f32[1024]{0:T(1024)}, u32[]{:S(2)}) copy-start(f32[1024]{0:T(1024)} %param.10) | copy-start | bytes 12292
  7.2 187.8 %all-reduce.20.cloned.1.call-start = ((), (), s32[]{:S(2)}) async-start(), calls=%async_computation.5 | async-start | bytes 2097152 | tf_op jit(solution)/shard_map/psum | solution.py:18
  7.2 53.1 %collective-permute-start = (f32[1024,256]{1,0:T(8,128)}, f32[1024,256]{1,0:T(8,128)}, u32[]{:S(2)}, u32[]{:S(2)}) collective-permute-start(f32[1024,256]{1,0:T(8,128)} %param.9), channel_id=1, source_target_pairs={{0,64},{16,80},{32,96},{48,112},{64,0},{80,16},{96,32},{112,48},{1... | collective-permute-start | bytes 3145736 | tf_op jit(solution)/shard_map/ppermute | solution.py:13
  62.1 1.2 copy-start.5
  70.4 125.7 %copy-start = (f32[1024,512]{0,1:T(8,128)}, f32[1024,512]{0,1:T(8,128)S(1)}, u32[]{:S(2)}) copy-start(f32[1024,512]{0,1:T(8,128)S(1)} %copy.28) | copy-start | bytes 6291460
  71.6 203.7 %all-reduce.10.cloned.1.call-start = ((), (), s32[]{:S(2)}) async-start(), calls=%async_computation | async-start | bytes 524288 | tf_op jit(solution)/shard_map/psum | solution.py:92
  198.0 220.5 %all-reduce.12.cloned.1.call-start = ((), (), s32[]{:S(2)}) async-start(), calls=%async_computation.1 | async-start | bytes 1048576 | tf_op jit(solution)/shard_map/psum | solution.py:18
  208.7 129.3 %copy-start.4 = (f32[1024,128]{0,1:T(8,128)S(1)}, f32[1024,128]{0,1:T(8,128)}, u32[]{:S(2)}) copy-start(f32[1024,128]{0,1:T(8,128)} %get-tuple-element.45) | copy-start | bytes 1572868
  277.4 61.3 %copy-start.3 = (f32[1024,128]{0,1:T(8,128)S(1)}, f32[1024,128]{0,1:T(8,128)}, u32[]{:S(2)}) copy-start(f32[1024,128]{0,1:T(8,128)} %get-tuple-element.46) | copy-start | bytes 1572868
  339.9 82.4 %copy-start.1 = (f32[1024,128]{0,1:T(8,128)}, f32[1024,128]{0,1:T(8,128)S(1)}, u32[]{:S(2)}) copy-start(f32[1024,128]{0,1:T(8,128)S(1)} %fusion.25) | copy-start | bytes 1572868
  340.9 199.3 %all-reduce.18.cloned.1.call-start = ((), (), s32[]{:S(2)}) async-start(), calls=%async_computation.4 | async-start | bytes 2097152 | tf_op jit(solution)/shard_map/psum | solution.py:18
  423.4 197.2 %all-reduce.14.cloned.1.call-start = ((), (), s32[]{:S(2)}) async-start(), calls=%async_computation.2 | async-start | bytes 524288 | tf_op jit(solution)/shard_map/psum | solution.py:92
  543.2 223.1 %all-reduce.16.cloned.1.call-start = ((), (), s32[]{:S(2)}) async-start(), calls=%async_computation.3 | async-start | bytes 1048576 | tf_op jit(solution)/shard_map/psum | solution.py:18
  686.9 0.8 copy-start.2
Sparse Core Ops, SparseCore 0:
  71.7 123.1 all-reduce.19
  198.1 77.2 all-reduce.9
  341.0 77.3 all-reduce.11
  423.5 116.6 all-reduce.17
  543.3 77.2 all-reduce.13
  688.8 77.3 all-reduce.15
where the time goes:
time: 789 us; the launch traced here: 781 us
  waiting for transfers between devices  558 us (71%)
  other arithmetic  123 us (16%)
  between operations  37.4 us (5%)
  local copies, waits for them, and re-layouts  30.3 us (4%)
  matrix products  23.5 us (3%)
  starting transfers between devices  8.41 us (1%)
    psum x4, waiting for transfers between devices, broadcast(): return lax.psum(jnp.where(mine, shard, jnp.zeros_like(shard)), axis)  393 us
    psum x2, waiting for transfers between devices, per_device(): pivot_block = lax.psum(jnp.concatenate(owned_rows, axis=0), 'row')  135 us
    another operation x14, other arithmetic, per_device(): lower_factor = jnp.linalg.cholesky(pivot_block)  69.3 us
    another operation x7, other arithmetic, per_device(): lax.linalg.triangular_solve(lower_factor, panel_cols, left_side=False, lo...  39.6 us
    ppermute x1, waiting for transfers between devices, swapped(): lax.ppermute(shard, axis, [(i, i ^ 1 << bit) for i in range(lax.axis_size...  30 us
  transfers between devices with their start and end apart: 7, of which 7 were waited for; matrix products, arithmetic and copies ran while one was open for 2% of the time, Pallas kernels for 0%

commit v1 on v0

--- a/solution.py
+++ b/solution.py
@@ -89,7 +89,7 @@
         for block_id in chosen:
             rows_here = lax.dynamic_slice_in_dim(panel_cols, block_id // row_count * BLK, BLK, 0)
             owned_rows.append(jnp.where(block_id % row_count == row_index, rows_here, 0.0))
-        pivot_block = lax.psum(jnp.concatenate(owned_rows, axis=0), "row")
+        pivot_block = jnp.sum(lax.all_gather(jnp.concatenate(owned_rows, axis=0), "row"), axis=0)
         lower_factor = jnp.linalg.cholesky(pivot_block)
         factor = lax.linalg.triangular_solve(
             lower_factor, panel_cols, left_side=False, lower=True, transpose_a=True

time: 789 us -> 717 us (0.909)
  waiting for transfers between devices: 558 us -> 490 us
    psum x2 -> x0, waiting for transfers between devices: 135 us -> none  [per_device(): pivot_block = lax.psum(jnp.concatenate(owned_rows, axis=0), 'row')]
    all_gather x0 -> x2, waiting for transfers between devices: none -> 66.3 us  [per_device(): lax.all_gather(jnp.concatenate(owned_rows, axis=0), 'row')]
where the time goes in v1:
time: 717 us; the launch traced here: 710 us
  waiting for transfers between devices  490 us (68%)
  other arithmetic  125 us (17%)
  between operations  38.1 us (5%)
  matrix products  24.7 us (3%)
  local copies, waits for them, and re-layouts  23.5 us (3%)
  starting transfers between devices  8.41 us (1%)
    psum x4, waiting for transfers between devices, broadcast(): return lax.psum(jnp.where(mine, shard, jnp.zeros_like(shard)), axis)  394 us
    another operation x14, other arithmetic, per_device(): lower_factor = jnp.linalg.cholesky(pivot_block)  69.3 us
    all_gather x2, waiting for transfers between devices, per_device(): lax.all_gather(jnp.concatenate(owned_rows, axis=0), 'row')  66.3 us
    another operation x7, other arithmetic, per_device(): lax.linalg.triangular_solve(lower_factor, panel_cols, left_side=False, lo...  39.6 us
    ppermute x1, waiting for transfers between devices, swapped(): lax.ppermute(shard, axis, [(i, i ^ 1 << bit) for i in range(lax.axis_size...  29.6 us
  transfers between devices with their start and end apart: 7, of which 7 were waited for; matrix products, arithmetic and copies ran while one was open for 2% of the time, Pallas kernels for 0%

profile of v1, /device:TPU:2, one launch (start us, length us, event | category | flops | bytes accessed | tf_op | source)
XLA Modules:
  0.0 709.9 jit_solution(13101470090596261503)
XLA Ops:
  7.2 7.7 %collective-permute-start = (f32[1024,256]{1,0:T(8,128)}, f32[1024,256]{1,0:T(8,128)}, u32[]{:S(2)}, u32[]{:S(2)}) collective-permute-start(f32[1024,256]{1,0:T(8,128)} %param.9), channel_id=1, source_target_pairs={{0,64},{16,80},{32,96},{48,112},{64,0},{80,16},{96,32},{112,48},{1... | collective-permute-start | bytes 3145736 | tf_op jit(solution)/shard_map/ppermute | solution.py:13
  17.5 1.5 fusion.61
  19.0 1.7 reshape.126
  26.3 1.0 broadcast_multiply_fusion
  27.3 1.2 fusion.5
  28.4 2.3 fusion.3
  30.8 29.6 %collective-permute-done = f32[1024,256]{1,0:T(8,128)} collective-permute-done((f32[1024,256]{1,0:T(8,128)}, f32[1024,256]{1,0:T(8,128)}, u32[]{:S(2)}, u32[]{:S(2)}) %collective-permute-start) | collective-permute-done | bytes 1048608 | tf_op jit(solution)/shard_map/ppermute | solution.py:13
  60.4 1.7 reshape.187
  62.1 1.2 fusion
  63.3 3.7 bitcast_add_fusion
  67.2 1.1 copy-done
  68.3 1.1 dynamic-slice_select_fusion.2
  69.6 123.2 %all-reduce.14.cloned.1.call-done = (f32[1024,128]{1,0:T(8,128)}, f32[1024,128]{1,0:T(8,128)}) async-done(((f32[1024,128]{1,0:T(8,128)}, f32[1024,128]{1,0:T(8,128)}), (f32[1024,128]{1,0:T(8,128)}, f32[1024,128]{1,0:T(8,128)})) %all-reduce.14.cloned.1.call-update) | async-done | bytes 1048592 | tf_op jit(solution)/shard_map/psum | solution.py:18
  192.8 1.1 constant_dynamic-update-slice_fusion.3
  193.9 1.1 constant_dynamic-update-slice_fusion.2
  211.9 1.3 or_select_fusion.2
  213.2 25.9 %all-gather.5.cloned.1.call-done = f32[2048,256]{1,0:T(8,128)} async-done(((f32[256,256]{1,0:T(8,128)}), f32[2048,256]{1,0:T(8,128)}) %all-gather.5.cloned.1.call-update) | async-done | bytes 2097168 | tf_op jit(solution)/shard_map/all_gather | solution.py:92
  239.0 1.8 reduce_sum.18
  241.0 11.7 %cholesky.130 = f32[128,128]{1,0:T(8,128)S(1)} custom-call(f32[128,128]{1,0:T(8,128)S(1)} %cholesky.194), custom_call_target="Cholesky" | custom-call | tf_op jit(solution)/shard_map/jit(cholesky)/cholesky | solution.py:93
  252.8 9.8 %custom-call.13 = f32[1,128,128]{1,2,0:T(8,128)S(1)} custom-call(f32[1,128,128]{2,1,0:T(8,128)S(1)} %get-tuple-element.70), custom_call_target="InvertDiagBlocksLowerTriangular" | custom-call | tf_op jit(solution)/shard_map/jit(cholesky)/cholesky | solution.py:93
  263.1 11.7 %cholesky.147 = f32[128,128]{1,0:T(8,128)S(1)} custom-call(f32[128,128]{1,0:T(8,128)S(1)} %convolution_subtract_fusion.3), custom_call_target="Cholesky" | custom-call | tf_op jit(solution)/shard_map/jit(cholesky)/cholesky | solution.py:93
  277.5 4.1 while.4
  278.4 1.3 bitcast_dynamic-update-slice_fusion.4
  280.3 1.3 bitcast_dynamic-update-slice_fusion.4
  281.6 19.7 %custom-call.14 = f32[2,128,128]{1,2,0:T(8,128)S(1)} custom-call(f32[2,128,128]{2,1,0:T(8,128)S(1)} %get-tuple-element.19), custom_call_target="InvertDiagBlocksLowerTriangular" | custom-call | tf_op jit(solution)/shard_map/triangular_solve/custom-call.0 | solution.py:94
  302.0 1.0 convolution_subtract_fusion.1
  304.7 1.3 or_select_fusion.3
  306.1 76.5 %all-reduce.8.cloned.1.call-done = f32[512,256]{0,1:T(8,128)} async-done(((f32[512,256]{0,1:T(8,128)}), f32[512,256]{0,1:T(8,128)}) %all-reduce.8.cloned.1.call-update) | async-done | bytes 524304 | tf_op jit(solution)/shard_map/psum | solution.py:18
  382.6 4.0 multiply_multiply_fusion.1
  386.7 1.1 dynamic-slice_select_fusion.1
  387.9 116.9 %all-reduce.12.cloned.1.call-done = (f32[1024,128]{1,0:T(8,128)}, f32[1024,128]{1,0:T(8,128)}) async-done(((f32[1024,128]{1,0:T(8,128)}, f32[1024,128]{1,0:T(8,128)}), (f32[1024,128]{1,0:T(8,128)}, f32[1024,128]{1,0:T(8,128)})) %all-reduce.12.cloned.1.call-update) | async-done | bytes 1048592 | tf_op jit(solution)/shard_map/psum | solution.py:18
  504.8 1.1 constant_dynamic-update-slice_fusion.5
  505.9 1.1 constant_dynamic-update-slice_fusion.4
  508.1 1.2 or_select_fusion
  509.3 1.2 or_select_fusion.1
  510.6 40.4 %all-gather.7.cloned.1.call-done = f32[2048,256]{1,0:T(8,128)} async-done(((f32[256,256]{1,0:T(8,128)}), f32[2048,256]{1,0:T(8,128)}) %all-gather.7.cloned.1.call-update) | async-done | bytes 2097168 | tf_op jit(solution)/shard_map/all_gather | solution.py:92
  551.0 1.8 reduce_sum.19
  553.0 11.7 %cholesky.164 = f32[128,128]{1,0:T(8,128)S(1)} custom-call(f32[128,128]{1,0:T(8,128)S(1)} %cholesky.197), custom_call_target="Cholesky" | custom-call | tf_op jit(solution)/shard_map/jit(cholesky)/cholesky | solution.py:93
  564.7 9.8 %custom-call.15 = f32[1,128,128]{1,2,0:T(8,128)S(1)} custom-call(f32[1,128,128]{2,1,0:T(8,128)S(1)} %get-tuple-element.66), custom_call_target="InvertDiagBlocksLowerTriangular" | custom-call | tf_op jit(solution)/shard_map/jit(cholesky)/cholesky | solution.py:93
  575.0 11.7 %cholesky.181 = f32[128,128]{1,0:T(8,128)S(1)} custom-call(f32[128,128]{1,0:T(8,128)S(1)} %convolution_subtract_fusion.2), custom_call_target="Cholesky" | custom-call | tf_op jit(solution)/shard_map/jit(cholesky)/cholesky | solution.py:93
  589.5 4.4 while.5
  590.4 1.4 bitcast_dynamic-update-slice_fusion.5
  592.5 1.4 bitcast_dynamic-update-slice_fusion.5
  593.9 19.7 %custom-call.16 = f32[2,128,128]{1,2,0:T(8,128)S(1)} custom-call(f32[2,128,128]{2,1,0:T(8,128)S(1)} %get-tuple-element.20), custom_call_target="InvertDiagBlocksLowerTriangular" | custom-call | tf_op jit(solution)/shard_map/triangular_solve/custom-call.0 | solution.py:94
  613.6 1.7 fusion.22
  615.3 2.0 convolution_subtract_fusion
  620.6 77.2 %all-reduce.10.cloned.1.call-done = f32[512,256]{0,1:T(8,128)} async-done(((f32[512,256]{0,1:T(8,128)}), f32[512,256]{0,1:T(8,128)}) %all-reduce.10.cloned.1.call-update) | async-done | bytes 524304 | tf_op jit(solution)/shard_map/psum | solution.py:18
  697.8 4.8 multiply_multiply_fusion
  (94 shorter events, 18.4 us)
Async XLA Ops:
  7.2 19.1 %copy-start.6 = (f32[1024]{0:T(1024)S(1)}, f32[1024]{0:T(1024)}, u32[]{:S(2)}) copy-start(f32[1024]{0:T(1024)} %param.10) | copy-start | bytes 12292
  7.2 185.6 %all-reduce.14.cloned.1.call-start = ((), (), s32[]{:S(2)}) async-start(), calls=%async_computation.5 | async-start | bytes 2097152 | tf_op jit(solution)/shard_map/psum | solution.py:18
  7.2 53.1 %collective-permute-start = (f32[1024,256]{1,0:T(8,128)}, f32[1024,256]{1,0:T(8,128)}, u32[]{:S(2)}, u32[]{:S(2)}) collective-permute-start(f32[1024,256]{1,0:T(8,128)} %param.9), channel_id=1, source_target_pairs={{0,64},{16,80},{32,96},{48,112},{64,0},{80,16},{96,32},{112,48},{1... | collective-permute-start | bytes 3145736 | tf_op jit(solution)/shard_map/ppermute | solution.py:13
  62.1 1.2 copy-start.5
  67.0 1.3 copy-start
  69.5 169.6 %all-gather.5.cloned.1.call-start = ((), (), s32[]{:S(2)}) async-start(), calls=%async_computation.2 | async-start | bytes 2359296 | tf_op jit(solution)/shard_map/all_gather | solution.py:92
  195.8 186.8 %all-reduce.8.cloned.1.call-start = ((), (), s32[]{:S(2)}) async-start(), calls=%async_computation | async-start | bytes 1048576 | tf_op jit(solution)/shard_map/psum | solution.py:18
  240.8 60.5 %copy-start.4 = (f32[1024,128]{1,0:T(8,128)S(1)}, f32[1024,128]{1,0:T(8,128)}, u32[]{:S(2)}) copy-start(f32[1024,128]{1,0:T(8,128)} %get-tuple-element.41) | copy-start | bytes 1572868
  241.0 61.0 %copy-start.3 = (f32[1024,128]{1,0:T(8,128)S(1)}, f32[1024,128]{1,0:T(8,128)}, u32[]{:S(2)}) copy-start(f32[1024,128]{1,0:T(8,128)} %get-tuple-element.42) | copy-start | bytes 1572868
  303.6 83.0 %copy-start.1 = (f32[1024,128]{0,1:T(8,128)}, f32[1024,128]{0,1:T(8,128)S(1)}, u32[]{:S(2)}) copy-start(f32[1024,128]{0,1:T(8,128)S(1)} %fusion.25) | copy-start | bytes 1572868
  304.6 200.2 %all-reduce.12.cloned.1.call-start = ((), (), s32[]{:S(2)}) async-start(), calls=%async_computation.4 | async-start | bytes 2097152 | tf_op jit(solution)/shard_map/psum | solution.py:18
  387.8 163.2 %all-gather.7.cloned.1.call-start = ((), (), s32[]{:S(2)}) async-start(), calls=%async_computation.3 | async-start | bytes 2359296 | tf_op jit(solution)/shard_map/all_gather | solution.py:92
  507.8 190.0 %all-reduce.10.cloned.1.call-start = ((), (), s32[]{:S(2)}) async-start(), calls=%async_computation.1 | async-start | bytes 1048576 | tf_op jit(solution)/shard_map/psum | solution.py:18
  618.0 0.8 copy-start.2
Sparse Core Ops, SparseCore 0:
  69.6 123.1 all-reduce.13
  195.9 43.0 all-gather.4
  304.7 77.8 all-reduce.7
  387.9 116.8 all-reduce.11
  507.9 43.0 all-gather.6
  619.9 77.8 all-reduce.9
